TPU v7x, 32 devices: a whole 2x2x4 slice. The times are simulated.
32 devices in a mesh: gx: 4 (over x, core), gy: 8 (over z, y).
Axes of the slice: x: 2, y: 2, z: 4, core: 2. Of those that a mesh axis runs over, the one named last changes fastest.
Arguments:
- field: float32 [12, 64, 64, 128], P(None, 'gx', 'gy'), may hold values from -16 to 16
- diffusion: float32 [12], replicated, may hold values from 0.02 to 0.15
- prefactor: float32 [12], replicated, may hold values from 0.05 to 0.3
- activation: float32 [12], replicated, may hold values from 0.5 to 2
- mixing: float32 [12, 12], replicated, may hold values from -1.75 to 1.75
- basis_x: float32 [64, 64], P('gx'), may hold values from -1 to 1, as said below
- basis_y: float32 [64, 64], P('gy'), may hold values from -1 to 1, as said below
- basis_z: float32 [128, 32], replicated, may hold values from -1 to 1, as said below
- basis_v: float32 [12, 6], replicated, may hold values from -1 to 1, as said below
Outputs:
- state: float32 [12, 64, 64, 128], P(None, 'gx', 'gy')
- recon: float32 [12, 64, 64, 128], P(None, 'gx', 'gy')
- residual: float32 [12], replicated
Inputs may be any that keep to these rules, and one draw needn't show every extreme that they name: `basis_x`: its 64 columns are mutually orthogonal, each of norm between 0.5 and 1. `basis_y`: its 64 columns are orthonormal. `basis_z`: its 32 columns are orthonormal. `basis_v`: its 6 columns are orthonormal.
All inputs are finite; a program needn't handle non-finite values.
Results may differ from a plain program's by a relative error of at most 0.00013.
Values sent between devices are 32-bit elements; how exact they have to be, the bound alone decides.
No kernel may reach another device: no remote copies, remote signals or barrier semaphores. Data moves between devices by JAX's collectives and lax.ppermute only.
A program may use at most 64 MiB of HBM per device.

v0:
```python
import jax
import jax.numpy as jnp
from jax import lax
from jax.sharding import PartitionSpec as P

HIGH = lax.Precision.HIGHEST


def padded_2(array, sides, width):
    for axis, dim in sides:
        peers, length = (lax.axis_size(axis), array.shape[dim])
        up = [(i, (i + 1) % peers) for i in range(peers - 1)]
        down = [(j, i) for i, j in up]
        last = lax.slice_in_dim(array, length - width, length, axis=dim)
        first = lax.slice_in_dim(array, 0, width, axis=dim)
        before = lax.ppermute(last, axis, up)
        after = lax.ppermute(first, axis, down)
        array = jnp.concatenate([before, array, after], axis=dim)
    return array


def lap_core(padded):
    centre = padded[:, 1:-1, 1:-1, 1:-1]
    summed = padded[:, 2:, 1:-1, 1:-1] + padded[:, :-2, 1:-1, 1:-1]
    summed = summed + padded[:, 1:-1, 2:, 1:-1] + padded[:, 1:-1, :-2, 1:-1]
    summed = summed + padded[:, 1:-1, 1:-1, 2:] + padded[:, 1:-1, 1:-1, :-2]
    return summed - 6.0 * centre


def reaction(centre, coeffs):
    diffusion, prefactor, activation, mixing = coeffs
    temper = 1.5 + jnp.tanh(centre[0])
    rate_terms = (
        prefactor[:, None, None, None]
        * jnp.exp(-activation[:, None, None, None] / temper[None])
        * centre
    )
    return jnp.einsum("vw,wxyz->vxyz", mixing, rate_terms, precision=HIGH)


def tendency(rimmed, centre, coeffs):
    padded = jnp.pad(rimmed, ((0, 0), (0, 0), (0, 0), (1, 1)))
    return coeffs[0][:, None, None, None] * lap_core(padded) + reaction(centre, coeffs)


def inside_mask(rows_x, rows_y):
    pos_x = lax.axis_index("gx") * rows_x + jnp.arange(rows_x + 2) - 1
    pos_y = lax.axis_index("gy") * rows_y + jnp.arange(rows_y + 2) - 1
    in_x = (pos_x >= 0) & (pos_x < rows_x * lax.axis_size("gx"))
    in_y = (pos_y >= 0) & (pos_y < rows_y * lax.axis_size("gy"))
    return in_x[:, None] & in_y[None, :]


def step_deep(state, coeffs, inside):
    wide = padded_2(state, (("gx", 1), ("gy", 2)), 2)
    centre = wide[:, 1:-1, 1:-1]
    section_wide = centre + tendency(wide, centre, coeffs)
    section_wide = jnp.where(inside[None, :, :, None], section_wide, 0.0)
    section = section_wide[:, 1:-1, 1:-1]
    return 0.5 * (state + section + tendency(section_wide, section, coeffs))


def on_device(field, diffusion, prefactor, activation, mixing, basis_x, basis_y, basis_z, basis_v):
    coeffs = (diffusion, prefactor, activation, mixing)
    rows_x = field.shape[1]
    rows_y = field.shape[2]
    state = field
    inside = inside_mask(rows_x, rows_y)
    state = step_deep(state, coeffs, inside)
    rank_z = basis_z.shape[1]
    rank_v = basis_v.shape[1]
    width = rank_z * rank_v
    proj_z = jnp.einsum("vxyz,zr->vxyr", state, basis_z, precision=HIGH)
    packed = jnp.einsum("vxyr,vs->xyrs", proj_z, basis_v, precision=HIGH)
    packed = packed.reshape(rows_x, rows_y, width)
    columns = basis_x
    part_x = lax.psum_scatter(
        jnp.einsum("xa,xyk->ayk", columns, packed, precision=HIGH),
        "gx",
        scatter_dimension=0,
        tiled=True,
    )
    core_block = jnp.einsum("ayk,yb->abk", part_x, basis_y, precision=HIGH)
    core_block = lax.psum(core_block, "gy")
    mixed_y = jnp.einsum("abk,yb->ayk", core_block, basis_y, precision=HIGH)
    columns = basis_x
    decoded = jnp.einsum(
        "xa,ayk->xyk", columns, lax.all_gather(mixed_y, "gx", axis=0, tiled=True), precision=HIGH
    )
    decoded = decoded.reshape(rows_x, rows_y, rank_z, rank_v)
    back_v = jnp.einsum("xyrs,vs->vxyr", decoded, basis_v, precision=HIGH)
    recon = jnp.einsum("vxyr,zr->vxyz", back_v, basis_z, precision=HIGH)
    error = state - recon
    miss_local = jnp.sum(error * error, axis=(1, 2, 3))
    mass_local = jnp.sum(state * state, axis=(1, 2, 3))
    miss, mass = lax.psum((miss_local, mass_local), ("gx", "gy"))
    residual = jnp.sqrt(miss / (mass + 1e-06))
    return (state, recon, residual)


def solution(mesh):
    return jax.shard_map(
        on_device,
        mesh=mesh,
        in_specs=(
            P(None, "gx", "gy", None),
            P(),
            P(),
            P(),
            P(),
            P("gx", None),
            P("gy", None),
            P(),
            P(),
        ),
        out_specs=(P(None, "gx", "gy", None), P(None, "gx", "gy", None), P()),
        check_vma=False,
    )
```

profile of v0, /device:TPU:0, one launch (start us, length us, event | category | flops | bytes accessed | tf_op | source)
XLA Modules:
  0.0 209.1 jit_solution(7740615977400366910)
XLA Ops:
  7.2 0.0 copy-start
  7.2 0.0 reduce-scatter.2.cloned.1.call-start
  7.2 1.0 fusion.57
  8.3 2.4 %collective-permute-start = (f32[12,2,8,128]{3,0,2,1:T(8,128)S(1)}, f32[12,2,8,128]{3,0,2,1:T(8,128)S(1)}, u32[]{:S(2)}, u32[]{:S(2)}) collective-permute-start(f32[12,2,8,128]{3,0,2,1:T(8,128)S(1)} %copy.76), channel_id=1, source_target_pairs={{0,8},{8,16},{16,24},{1,9},{9,17},{17,25},{2,10},{10,18},{18,26},{... | collective-permute-start | bytes 294920 | tf_op jit(solution)/shard_map/ppermute | solution.py:16
  10.8 1.3 collective-permute-start.1
  12.1 0.0 collective-permute-done
  12.1 0.0 copy-start.7
  12.1 0.5 copy_dynamic-update-slice_fusion
  12.6 3.5 %collective-permute-done.1 = f32[12,2,8,128]{3,0,2,1:T(8,128)S(1)} collective-permute-done((f32[12,2,8,128]{3,0,2,1:T(8,128)S(1)}, f32[12,2,8,128]{3,0,2,1:T(8,128)S(1)}, u32[]{:S(2)}, u32[]{:S(2)}) %collective-permute-start.1) | collective-permute-done | bytes 98336 | tf_op jit(solution)/shard_map/ppermute | solution.py:17
  16.2 3.4 %collective-permute-start.2 = (f32[12,20,2,128]{3,0,2,1:T(8,128)S(1)}, f32[12,20,2,128]{3,0,2,1:T(8,128)S(1)}, u32[]{:S(2)}, u32[]{:S(2)}) collective-permute-start(f32[12,20,2,128]{3,0,2,1:T(8,128)S(1)} %get-tuple-element.19), channel_id=1, source_target_pairs={{0,1},{1,2},{2,3},{3,4},{4,5},{5,6},{6,7},{8,9},{9,10},{10,11},{11... | collective-permute-start | bytes 737288 | tf_op jit(solution)/shard_map/ppermute | solution.py:16
  19.6 1.3 collective-permute-start.3
  20.9 0.0 copy-done.7
  20.9 0.1 broadcast_and_fusion
  21.0 4.2 %collective-permute-done.2 = f32[12,20,2,128]{3,0,2,1:T(8,128)S(1)} collective-permute-done((f32[12,20,2,128]{3,0,2,1:T(8,128)S(1)}, f32[12,20,2,128]{3,0,2,1:T(8,128)S(1)}, u32[]{:S(2)}, u32[]{:S(2)}) %collective-permute-start.2) | collective-permute-done | bytes 245792 | tf_op jit(solution)/shard_map/ppermute | solution.py:16
  25.2 4.6 %collective-permute-done.3 = f32[12,20,2,128]{3,0,2,1:T(8,128)S(1)} collective-permute-done((f32[12,20,2,128]{3,0,2,1:T(8,128)S(1)}, f32[12,20,2,128]{3,0,2,1:T(8,128)S(1)}, u32[]{:S(2)}, u32[]{:S(2)}) %collective-permute-start.3) | collective-permute-done | bytes 245792 | tf_op jit(solution)/shard_map/ppermute | solution.py:17
  29.8 0.2 pad_maximum_fusion
  30.0 0.1 fusion.41
  30.1 2.3 %fusion.8 = f32[12,18,10,128]{3,0,2,1:T(8,128)S(1)} fusion(f32[12,20,12,128]{3,0,2,1:T(8,128)S(1)} %pad_maximum_fusion, f32[12,20,8,128]{3,0,2,1:T(8,128)S(1)} %constant_dynamic-update-slice_fusion, f32[12,20,2,128]{3,0,2,1:T(8,128)S(1)} %collective-permute-done.2, f32[12,20,2,128]{3,0,2,1:T(8,128)S(1)} %collective-permute-done.3, ...), kind=kOutput, calls=%fused_computation.14 | convolution fusion | flops 44236800 | bytes 11096576 | tf_op jit(solution)/shard_map/vw,wxyz->vxyz/dot_general | solution.py:38
  32.5 0.1 fusion.42
  32.6 2.2 %fusion.23 = f32[12,16,8,128]{3,0,2,1:T(8,128)S(1)} fusion(f32[12,18,10,128]{3,0,2,1:T(8,128)S(1)} %fusion.8, f32[16,8,128]{2,1,0:T(8,128)S(1)} %bitcast.62, f32[12]{0:T(128)S(1)} %neg.5, f32[12]{0:T(128)S(1)} %copy-done.8, f32[12]{0:T(128)S(1)} %copy-done.9, f32[12,16,8,128]{3,2,1,0:T(8,128)S(1)} %copy-done.2, f32[12,12]{1,0:T(8,128)S(1)} %copy-done.6), kind=kOutput, calls=%fused_computation.37 | convolution fusion | flops 31260672 | bytes 9414144 | tf_op jit(solution)/shard_map/vw,wxyz->vxyz/dot_general | solution.py:38
  34.8 0.0 copy-start.5
  34.8 1.0 fusion.44
  35.8 0.0 copy-done.5
  35.8 0.0 copy-start.3
  35.8 0.7 fusion.51
  36.5 0.5 copy.49
  37.1 0.0 copy-start.4
  37.1 1.7 convolution_bitcast_fusion.3
  38.7 1.1 copy.51
  39.8 0.0 reduce-scatter.2.cloned.1.call-update
  39.9 0.0 all-reduce.5.cloned.1.call-start
  39.9 27.8 %reduce-scatter.2.cloned.1.call-done = f32[16,8,192]{2,1,0:T(8,128)} async-done(((f32[64,8,192]{2,1,0:T(8,128)}), f32[16,8,192]{2,1,0:T(8,128)}) %reduce-scatter.2.cloned.1.call-update) | async-done | bytes 98320 | tf_op jit(solution)/shard_map/reduce_scatter | solution.py:77
  67.7 0.0 copy-done.4
  67.7 2.9 %convolution_bitcast_fusion.1 = f32[16,64,192]{2,1,0:T(8,128)} fusion(f32[16,8,192]{2,1,0:T(8,128)} %reduce-scatter.2.cloned.1.call-done, f32[8,64]{1,0:T(8,128)S(1)} %copy-done.4), kind=kOutput, calls=%fused_computation.23 | convolution fusion | flops 18874368 | bytes 886784 | tf_op jit(solution)/shard_map/ayk,yb->abk/dot_general | solution.py:83
  70.6 0.0 all-reduce.5.cloned.1.call-update
  70.6 1.1 copy.57
  71.7 77.8 %all-reduce.5.cloned.1.call-done = f32[16,64,192]{2,1,0:T(8,128)} async-done(((f32[16,64,192]{2,1,0:T(8,128)}), f32[16,64,192]{2,1,0:T(8,128)}) %all-reduce.5.cloned.1.call-update) | async-done | bytes 786448 | tf_op jit(solution)/shard_map/psum | solution.py:84
  149.5 1.9 convolution_bitcast_fusion.5
  151.3 7.3 %all_gather.3 = f32[64,8,192]{2,1,0:T(8,128)S(1)} all-gather(f32[16,8,192]{2,1,0:T(8,128)S(1)} %convolution_bitcast_fusion.5), channel_id=1, replica_groups=mesh['gx'=4,'gy'=8] {'gx'}, dimensions={0}, use_global_device_ids=true | all-gather | bytes 491520 | tf_op jit(solution)/shard_map/all_gather | solution.py:88
  158.7 0.5 convolution_bitcast_fusion.4
  159.2 0.3 copy.53
  159.5 0.6 copy.54
  160.1 1.0 convolution_bitcast_fusion
  161.2 0.9 fusion.31
  162.1 0.0 copy-start.1
  162.1 0.7 multiply_reduce_fusion
  162.8 38.9 %all-reduce.2 = (f32[12]{0:T(128)S(1)}, f32[12]{0:T(128)S(1)}) all-reduce(f32[12]{0:T(128)S(1)} %get-tuple-element.16, f32[12]{0:T(128)S(1)} %get-tuple-element.15), channel_id=1, replica_groups=mesh['gx'=4,'gy'=8] {'gx','gy'}, use_global_device_ids=true, to_apply=%region_3.4 | all-reduce | flops 24 | bytes 192 | tf_op jit(solution)/shard_map/psum | solution.py:96
  201.7 0.5 fusion.55
  (20 shorter events, 0.2 us)
Async XLA Ops:
  7.2 27.6 %copy-start = (f32[128,32]{0,1:T(8,128)S(1)}, f32[128,32]{0,1:T(8,128)}, u32[]{:S(2)}) copy-start(f32[128,32]{0,1:T(8,128)} %param.16) | copy-start | bytes 49156
  7.2 4.9 %copy-start.2 = (f32[12,16,8,128]{3,2,1,0:T(8,128)S(1)}, f32[12,16,8,128]{3,2,1,0:T(8,128)}, u32[]{:S(2)}) copy-start(f32[12,16,8,128]{3,2,1,0:T(8,128)} %param.9) | copy-start | bytes 2359300
  7.2 60.5 %reduce-scatter.2.cloned.1.call-start = ((), (), s32[]{:S(2)}) async-start(), calls=%async_computation.1 | async-start | bytes 655360 | tf_op jit(solution)/shard_map/reduce_scatter | solution.py:77
  8.3 3.8 %collective-permute-start = (f32[12,2,8,128]{3,0,2,1:T(8,128)S(1)}, f32[12,2,8,128]{3,0,2,1:T(8,128)S(1)}, u32[]{:S(2)}, u32[]{:S(2)}) collective-permute-start(f32[12,2,8,128]{3,0,2,1:T(8,128)S(1)} %copy.76), channel_id=1, source_target_pairs={{0,8},{8,16},{16,24},{1,9},{9,17},{17,25},{2,10},{10,18},{18,26},{... | collective-permute-start | bytes 294920 | tf_op jit(solution)/shard_map/ppermute | solution.py:16
  10.8 5.3 %collective-permute-start.1 = (f32[12,2,8,128]{3,0,2,1:T(8,128)S(1)}, f32[12,2,8,128]{3,0,2,1:T(8,128)S(1)}, u32[]{:S(2)}, u32[]{:S(2)}) collective-permute-start(f32[12,2,8,128]{3,0,2,1:T(8,128)S(1)} %copy.77), channel_id=1, source_target_pairs={{8,0},{16,8},{24,16},{9,1},{17,9},{25,17},{10,2},{18,10},{26,18},{... | collective-permute-start | bytes 294920 | tf_op jit(solution)/shard_map/ppermute | solution.py:17
  12.1 8.8 %copy-start.7 = (f32[12]{0:T(128)S(1)}, f32[12]{0:T(128)}, u32[]{:S(2)}) copy-start(f32[12]{0:T(128)} %param.12) | copy-start | bytes 148
  16.2 9.0 %collective-permute-start.2 = (f32[12,20,2,128]{3,0,2,1:T(8,128)S(1)}, f32[12,20,2,128]{3,0,2,1:T(8,128)S(1)}, u32[]{:S(2)}, u32[]{:S(2)}) collective-permute-start(f32[12,20,2,128]{3,0,2,1:T(8,128)S(1)} %get-tuple-element.19), channel_id=1, source_target_pairs={{0,1},{1,2},{2,3},{3,4},{4,5},{5,6},{6,7},{8,9},{9,10},{10,11},{11... | collective-permute-start | bytes 737288 | tf_op jit(solution)/shard_map/ppermute | solution.py:16
  19.6 10.2 %collective-permute-start.3 = (f32[12,20,2,128]{3,0,2,1:T(8,128)S(1)}, f32[12,20,2,128]{3,0,2,1:T(8,128)S(1)}, u32[]{:S(2)}, u32[]{:S(2)}) collective-permute-start(f32[12,20,2,128]{3,0,2,1:T(8,128)S(1)} %get-tuple-element.20), channel_id=1, source_target_pairs={{1,0},{2,1},{3,2},{4,3},{5,4},{6,5},{7,6},{9,8},{10,9},{11,10},{12... | collective-permute-start | bytes 737288 | tf_op jit(solution)/shard_map/ppermute | solution.py:17
  21.0 9.1 %copy-start.6 = (f32[12,12]{1,0:T(8,128)S(1)}, f32[12,12]{1,0:T(8,128)}, u32[]{:S(2)}) copy-start(f32[12,12]{1,0:T(8,128)} %param.13) | copy-start | bytes 1732
  21.0 9.1 %copy-start.8 = (f32[12]{0:T(128)S(1)}, f32[12]{0:T(128)}, u32[]{:S(2)}) copy-start(f32[12]{0:T(128)} %param.11) | copy-start | bytes 148
  21.0 9.1 %copy-start.9 = (f32[12]{0:T(128)S(1)}, f32[12]{0:T(128)}, u32[]{:S(2)}) copy-start(f32[12]{0:T(128)} %param.10) | copy-start | bytes 148
  34.8 1.0 copy-start.5
  35.8 1.3 copy-start.3
  37.1 30.6 %copy-start.4 = (f32[8,64]{1,0:T(8,128)S(1)}, f32[8,64]{1,0:T(8,128)}, u32[]{:S(2)}) copy-start(f32[8,64]{1,0:T(8,128)} %param.15) | copy-start | bytes 6148
  39.9 109.6 %all-reduce.5.cloned.1.call-start = ((), (), s32[]{:S(2)}) async-start(), calls=%async_computation.2 | async-start | bytes 2097152 | tf_op jit(solution)/shard_map/psum | solution.py:84
  162.1 40.1 %copy-start.1 = (f32[12,16,8,128]{3,2,1,0:T(8,128)}, f32[12,16,8,128]{3,2,1,0:T(8,128)S(1)}, u32[]{:S(2)}) copy-start(f32[12,16,8,128]{3,2,1,0:T(8,128)S(1)} %fusion.31) | copy-start | bytes 2359300
Sparse Core Ops, SparseCore 0:
  40.0 27.6 reduce-scatter.1
  71.2 78.2 all-reduce.4
where the time goes:
time: 209 us
  waiting for transfers between devices  118 us (56%)
  blocking collectives  46.3 us (22%)
  matrix products  15.1 us (7%)
  between operations  14.4 us (7%)
  starting transfers between devices  8.51 us (4%)
  local copies, waits for them, and re-layouts  5.35 us (3%)
    psum x1, waiting for transfers between devices, on_device(): core_block = lax.psum(core_block, 'gy')  77.8 us
    psum x1, blocking collectives, on_device(): miss, mass = lax.psum((miss_local, mass_local), ('gx', 'gy'))  38.9 us
    reduce_scatter x1, waiting for transfers between devices, on_device(): lax.psum_scatter(jnp.einsum('xa,xyk->ayk', columns, packed, precision=HIG...  27.8 us
    ppermute x2, waiting for transfers between devices, padded_2(): after = lax.ppermute(first, axis, down)  8.07 us
    all_gather x1, blocking collectives, on_device(): lax.all_gather(mixed_y, 'gx', axis=0, tiled=True)  7.32 us
    ppermute x2, starting transfers between devices, padded_2(): before = lax.ppermute(last, axis, up)  5.85 us
    dot_general x2, matrix products, reaction(): return jnp.einsum('vw,wxyz->vxyz', mixing, rate_terms, precision=HIGH)  4.55 us
  transfers between devices with their start and end apart: 6, of which 5 were waited for; matrix products, arithmetic and copies ran while one was open for 1% of the time, Pallas kernels for 0%

commit v1 on v0

--- a/solution.py
+++ b/solution.py
@@ -2,8 +2,10 @@
 import jax.numpy as jnp
 from jax import lax
 from jax.sharding import PartitionSpec as P
+from jax.lax import all_gather
 
 HIGH = lax.Precision.HIGHEST
+turn_the_marks = lambda load: all_gather(load, "gy").sum(axis=0)
 
 
 def padded_2(array, sides, width):
@@ -81,7 +83,7 @@
         tiled=True,
     )
     core_block = jnp.einsum("ayk,yb->abk", part_x, basis_y, precision=HIGH)
-    core_block = lax.psum(core_block, "gy")
+    core_block = turn_the_marks(core_block)
     mixed_y = jnp.einsum("abk,yb->ayk", core_block, basis_y, precision=HIGH)
     columns = basis_x
     decoded = jnp.einsum(

time: 209 us -> 258 us (1.23)
  waiting for transfers between devices: 118 us -> 164 us
  other arithmetic: 1.65 us -> 6.03 us
    all_gather x0 -> x1, waiting for transfers between devices: none -> 124 us  [turn_the_marks = lambda load: all_gather(load, 'gy').sum(axis=0)]
    psum x1 -> x0, waiting for transfers between devices: 77.8 us -> none  [on_device(): core_block = lax.psum(core_block, 'gy')]
    reduce_sum x0 -> x1, other arithmetic: none -> 4.38 us  [turn_the_marks = lambda load: all_gather(load, 'gy').sum(axis=0)]
where the time goes in v1:
time: 258 us; the launch traced here: 257 us
  waiting for transfers between devices  164 us (64%)
  blocking collectives  45.7 us (18%)
  matrix products  14.8 us (6%)
  between operations  14.4 us (6%)
  starting transfers between devices  8.51 us (3%)
  other arithmetic  6.03 us (2%)
  local copies, waits for them, and re-layouts  4.25 us (2%)
    all_gather x1, waiting for transfers between devices, turn_the_marks = lambda load: all_gather(load, 'gy').sum(axis=0)  124 us
    psum x1, blocking collectives, on_device(): miss, mass = lax.psum((miss_local, mass_local), ('gx', 'gy'))  38.4 us
    reduce_scatter x1, waiting for transfers between devices, on_device(): lax.psum_scatter(jnp.einsum('xa,xyk->ayk', columns, packed, precision=HIG...  27.8 us
    ppermute x2, waiting for transfers between devices, padded_2(): after = lax.ppermute(first, axis, down)  8.07 us
    all_gather x1, blocking collectives, on_device(): lax.all_gather(mixed_y, 'gx', axis=0, tiled=True)  7.32 us
    ppermute x2, starting transfers between devices, padded_2(): before = lax.ppermute(last, axis, up)  5.85 us
  transfers between devices with their start and end apart: 6, of which 5 were waited for; matrix products, arithmetic and copies ran while one was open for 1% of the time, Pallas kernels for 0%

profile of v1, /device:TPU:0, one launch (start us, length us, event | category | flops | bytes accessed | tf_op | source)
XLA Modules:
  0.0 257.2 jit_solution(7537983616450086570)
XLA Ops:
  7.2 0.0 copy-start
  7.2 0.0 copy-start.2
  7.2 0.0 reduce-scatter.2.cloned.1.call-start
  7.2 1.0 fusion.58
  8.3 2.4 collective-permute-start
  10.8 1.3 collective-permute-start.1
  12.1 0.0 collective-permute-done
  12.1 0.0 copy-start.7
  12.1 0.5 copy_dynamic-update-slice_fusion
  12.6 3.5 %collective-permute-done.1 = f32[12,2,8,128]{3,0,2,1:T(8,128)S(1)} collective-permute-done((f32[12,2,8,128]{3,0,2,1:T(8,128)S(1)}, f32[12,2,8,128]{3,0,2,1:T(8,128)S(1)}, u32[]{:S(2)}, u32[]{:S(2)}) %collective-permute-start.1) | collective-permute-done | bytes 98336 | tf_op jit(solution)/shard_map/ppermute | solution.py:19
  16.2 3.4 %collective-permute-start.2 = (f32[12,20,2,128]{3,0,2,1:T(8,128)S(1)}, f32[12,20,2,128]{3,0,2,1:T(8,128)S(1)}, u32[]{:S(2)}, u32[]{:S(2)}) collective-permute-start(f32[12,20,2,128]{3,0,2,1:T(8,128)S(1)} %get-tuple-element.19), channel_id=1, source_target_pairs={{0,1},{1,2},{2,3},{3,4},{4,5},{5,6},{6,7},{8,9},{9,10},{10,11},{11... | collective-permute-start | bytes 737288 | tf_op jit(solution)/shard_map/ppermute | solution.py:18
  19.6 1.3 collective-permute-start.3
  20.9 0.0 copy-done.7
  20.9 0.1 broadcast_and_fusion
  21.0 4.2 %collective-permute-done.2 = f32[12,20,2,128]{3,0,2,1:T(8,128)S(1)} collective-permute-done((f32[12,20,2,128]{3,0,2,1:T(8,128)S(1)}, f32[12,20,2,128]{3,0,2,1:T(8,128)S(1)}, u32[]{:S(2)}, u32[]{:S(2)}) %collective-permute-start.2) | collective-permute-done | bytes 245792 | tf_op jit(solution)/shard_map/ppermute | solution.py:18
  25.2 4.6 %collective-permute-done.3 = f32[12,20,2,128]{3,0,2,1:T(8,128)S(1)} collective-permute-done((f32[12,20,2,128]{3,0,2,1:T(8,128)S(1)}, f32[12,20,2,128]{3,0,2,1:T(8,128)S(1)}, u32[]{:S(2)}, u32[]{:S(2)}) %collective-permute-start.3) | collective-permute-done | bytes 245792 | tf_op jit(solution)/shard_map/ppermute | solution.py:19
  29.8 0.2 pad_maximum_fusion
  30.0 0.1 fusion.42
  30.1 2.3 fusion.8
  32.5 0.1 fusion.43
  32.6 2.2 fusion.23
  34.8 0.0 copy-start.5
  34.8 1.0 fusion.45
  35.8 0.0 copy-done.5
  35.8 0.0 copy-start.3
  35.8 0.7 fusion.52
  36.5 0.0 copy-start.4
  36.6 0.5 copy.49
  37.1 2.4 convolution_bitcast_fusion.3
  39.5 0.0 reduce-scatter.2.cloned.1.call-update
  39.6 0.0 all-gather.3.cloned.1.call-start
  39.6 27.8 %reduce-scatter.2.cloned.1.call-done = f32[16,8,192]{2,0,1:T(8,128)} async-done(((f32[64,8,192]{2,0,1:T(8,128)}), f32[16,8,192]{2,0,1:T(8,128)}) %reduce-scatter.2.cloned.1.call-update) | async-done | bytes 98320 | tf_op jit(solution)/shard_map/reduce_scatter | solution.py:79
  67.4 3.0 %convolution_bitcast_fusion.1 = f32[16,64,192]{2,1,0:T(8,128)} fusion(f32[16,8,192]{2,0,1:T(8,128)} %reduce-scatter.2.cloned.1.call-done, f32[8,64]{1,0:T(8,128)S(1)} %copy-done.4), kind=kOutput, calls=%fused_computation.23 | convolution fusion | flops 18874368 | bytes 886784 | tf_op jit(solution)/shard_map/ayk,yb->abk/dot_general | solution.py:85
  70.3 0.0 all-gather.3.cloned.1.call-update
  70.4 1.1 copy.57
  71.5 123.5 %all-gather.3.cloned.1.call-done = f32[128,64,192]{2,1,0:T(8,128)} async-done(((f32[16,64,192]{2,1,0:T(8,128)}), f32[128,64,192]{2,1,0:T(8,128)}) %all-gather.3.cloned.1.call-update) | async-done | bytes 6291472 | tf_op jit(solution)/shard_map/all_gather | solution.py:8
  195.0 4.4 %reduce_sum.27 = f32[16,64,192]{2,1,0:T(8,128)S(1)} reduce(f32[8,16,64,192]{3,2,1,0:T(8,128)} %bitcast.59, f32[]{:T(128)} %constant.6.clone.1), dimensions={0}, to_apply=%region_1.2 | reduce | flops 1376256 | bytes 7077892 | tf_op jit(solution)/shard_map/reduce_sum | solution.py:8
  199.4 0.7 convolution_bitcast_fusion.5
  200.0 7.3 %all_gather.11 = f32[64,8,192]{2,1,0:T(8,128)S(1)} all-gather(f32[16,8,192]{2,1,0:T(8,128)S(1)} %convolution_bitcast_fusion.5), channel_id=1, replica_groups=mesh['gx'=4,'gy'=8] {'gx'}, dimensions={0}, use_global_device_ids=true | all-gather | bytes 491520 | tf_op jit(solution)/shard_map/all_gather | solution.py:90
  207.3 0.5 convolution_bitcast_fusion.4
  207.9 0.3 copy.53
  208.2 0.6 copy.54
  208.8 1.0 convolution_bitcast_fusion
  209.8 0.9 fusion.31
  210.8 0.0 copy-start.1
  210.8 0.7 multiply_reduce_fusion
  211.5 38.4 %all-reduce.2 = (f32[12]{0:T(128)S(1)}, f32[12]{0:T(128)S(1)}) all-reduce(f32[12]{0:T(128)S(1)} %get-tuple-element.16, f32[12]{0:T(128)S(1)} %get-tuple-element.15), channel_id=1, replica_groups=mesh['gx'=4,'gy'=8] {'gx','gy'}, use_global_device_ids=true, to_apply=%region_3.4 | all-reduce | flops 24 | bytes 192 | tf_op jit(solution)/shard_map/psum | solution.py:98
  249.8 0.5 fusion.56
  (20 shorter events, 0.2 us)
Async XLA Ops:
  7.2 27.6 %copy-start = (f32[128,32]{0,1:T(8,128)S(1)}, f32[128,32]{0,1:T(8,128)}, u32[]{:S(2)}) copy-start(f32[128,32]{0,1:T(8,128)} %param.16) | copy-start | bytes 49156
  7.2 4.9 %copy-start.2 = (f32[12,16,8,128]{3,2,1,0:T(8,128)S(1)}, f32[12,16,8,128]{3,2,1,0:T(8,128)}, u32[]{:S(2)}) copy-start(f32[12,16,8,128]{3,2,1,0:T(8,128)} %param.9) | copy-start | bytes 2359300
  7.2 60.2 %reduce-scatter.2.cloned.1.call-start = ((), (), s32[]{:S(2)}) async-start(), calls=%async_computation.1 | async-start | bytes 655360 | tf_op jit(solution)/shard_map/reduce_scatter | solution.py:79
  8.3 3.8 %collective-permute-start = (f32[12,2,8,128]{3,0,2,1:T(8,128)S(1)}, f32[12,2,8,128]{3,0,2,1:T(8,128)S(1)}, u32[]{:S(2)}, u32[]{:S(2)}) collective-permute-start(f32[12,2,8,128]{3,0,2,1:T(8,128)S(1)} %copy.78), channel_id=1, source_target_pairs={{0,8},{8,16},{16,24},{1,9},{9,17},{17,25},{2,10},{10,18},{18,26},{... | collective-permute-start | bytes 294920 | tf_op jit(solution)/shard_map/ppermute | solution.py:18
  10.8 5.3 %collective-permute-start.1 = (f32[12,2,8,128]{3,0,2,1:T(8,128)S(1)}, f32[12,2,8,128]{3,0,2,1:T(8,128)S(1)}, u32[]{:S(2)}, u32[]{:S(2)}) collective-permute-start(f32[12,2,8,128]{3,0,2,1:T(8,128)S(1)} %copy.79), channel_id=1, source_target_pairs={{8,0},{16,8},{24,16},{9,1},{17,9},{25,17},{10,2},{18,10},{26,18},{... | collective-permute-start | bytes 294920 | tf_op jit(solution)/shard_map/ppermute | solution.py:19
  12.1 8.8 %copy-start.7 = (f32[12]{0:T(128)S(1)}, f32[12]{0:T(128)}, u32[]{:S(2)}) copy-start(f32[12]{0:T(128)} %param.12) | copy-start | bytes 148
  16.2 9.0 %collective-permute-start.2 = (f32[12,20,2,128]{3,0,2,1:T(8,128)S(1)}, f32[12,20,2,128]{3,0,2,1:T(8,128)S(1)}, u32[]{:S(2)}, u32[]{:S(2)}) collective-permute-start(f32[12,20,2,128]{3,0,2,1:T(8,128)S(1)} %get-tuple-element.19), channel_id=1, source_target_pairs={{0,1},{1,2},{2,3},{3,4},{4,5},{5,6},{6,7},{8,9},{9,10},{10,11},{11... | collective-permute-start | bytes 737288 | tf_op jit(solution)/shard_map/ppermute | solution.py:18
  19.6 10.2 %collective-permute-start.3 = (f32[12,20,2,128]{3,0,2,1:T(8,128)S(1)}, f32[12,20,2,128]{3,0,2,1:T(8,128)S(1)}, u32[]{:S(2)}, u32[]{:S(2)}) collective-permute-start(f32[12,20,2,128]{3,0,2,1:T(8,128)S(1)} %get-tuple-element.20), channel_id=1, source_target_pairs={{1,0},{2,1},{3,2},{4,3},{5,4},{6,5},{7,6},{9,8},{10,9},{11,10},{12... | collective-permute-start | bytes 737288 | tf_op jit(solution)/shard_map/ppermute | solution.py:19
  21.0 9.1 %copy-start.6 = (f32[12,12]{1,0:T(8,128)S(1)}, f32[12,12]{1,0:T(8,128)}, u32[]{:S(2)}) copy-start(f32[12,12]{1,0:T(8,128)} %param.13) | copy-start | bytes 1732
  21.0 9.1 %copy-start.8 = (f32[12]{0:T(128)S(1)}, f32[12]{0:T(128)}, u32[]{:S(2)}) copy-start(f32[12]{0:T(128)} %param.11) | copy-start | bytes 148
  21.0 9.1 %copy-start.9 = (f32[12]{0:T(128)S(1)}, f32[12]{0:T(128)}, u32[]{:S(2)}) copy-start(f32[12]{0:T(128)} %param.10) | copy-start | bytes 148
  34.8 1.0 copy-start.5
  35.8 1.3 copy-start.3
  36.5 30.8 %copy-start.4 = (f32[8,64]{1,0:T(8,128)S(1)}, f32[8,64]{1,0:T(8,128)}, u32[]{:S(2)}) copy-start(f32[8,64]{1,0:T(8,128)} %param.15) | copy-start | bytes 6148
  39.6 155.4 %all-gather.3.cloned.1.call-start = ((), (), s32[]{:S(2)}) async-start(), calls=%async_computation.2 | async-start | bytes 9437184 | tf_op jit(solution)/shard_map/all_gather | solution.py:8
  210.8 39.6 %copy-start.1 = (f32[12,16,8,128]{3,2,1,0:T(8,128)}, f32[12,16,8,128]{3,2,1,0:T(8,128)S(1)}, u32[]{:S(2)}) copy-start(f32[12,16,8,128]{3,2,1,0:T(8,128)S(1)} %fusion.31) | copy-start | bytes 2359300
Sparse Core Ops, SparseCore 0:
  39.7 27.6 reduce-scatter.1
  70.5 124.4 all-gather.2
